TPU v7x, 32 devices: a whole 2x2x4 slice. The times are simulated.
32 devices in a mesh: hid: 8 (over y, x, core), tok: 4 (over z).
Axes of the slice: x: 2, y: 2, z: 4, core: 2. Of those that a mesh axis runs over, the one named last changes fastest.
Arguments:
- tokens: bfloat16 [896, 8192], P('tok', 'hid'), may hold values from -6 to 6
- in_blocks: bfloat16 [128, 6, 256, 256], P('hid', None, 'tok'), may hold values from -0.15625 to 0.15625
- in_left: bfloat16 [8192, 256], P(('hid', 'tok')), may hold values from -0.0625 to 0.0625
- in_right: bfloat16 [256, 32768], P(None, ('hid', 'tok')), may hold values from -0.375 to 0.375
- in_lists: int32 [128, 6], replicated, may hold values from 0 to 31, as said below
- out_blocks: bfloat16 [128, 6, 256, 256], P('hid', None, 'tok'), may hold values from -0.078125 to 0.078125
- out_left: bfloat16 [32768, 256], P(('hid', 'tok')), may hold values from -0.03125 to 0.03125
- out_right: bfloat16 [256, 8192], P(None, ('hid', 'tok')), may hold values from -0.375 to 0.375
- out_lists: int32 [128, 6], replicated, may hold values from 0 to 31, as said below
- cotangent: bfloat16 [896, 8192], P('tok', 'hid'), may hold values from -6 to 6
Outputs:
- layer_out: bfloat16 [896, 8192], P('tok', 'hid')
- grad_tokens: bfloat16 [896, 8192], P('tok', 'hid')
- grad_in_blocks: bfloat16 [128, 6, 256, 256], P('hid', None, 'tok')
- grad_in_left: bfloat16 [8192, 256], P(('hid', 'tok'))
- grad_in_right: bfloat16 [256, 32768], P(None, ('hid', 'tok'))
- grad_out_blocks: bfloat16 [128, 6, 256, 256], P('hid', None, 'tok')
- grad_out_left: bfloat16 [32768, 256], P(('hid', 'tok'))
- grad_out_right: bfloat16 [256, 8192], P(None, ('hid', 'tok'))
Inputs may be any that keep to these rules, and one draw needn't show every extreme that they name: There is one whole number m, the same for every row, with in_lists[c, 0] = ((c * 8192) // 32768) XOR m, and in_lists[c, k] = in_lists[c, 0] XOR 2^(k-1) for k = 1 to 5. `out_lists`: the same butterfly form as in_lists, with its own number m, which differs from that of in_lists.
All inputs are finite; a program needn't handle non-finite values.
Results may differ from a plain program's by a relative error of at most 0.012.
Values may be sent and summed in bfloat16 or wider, within the bound.
A program may use at most 256 MiB of HBM per device.

v0:
```python
import jax
import jax.numpy as jnp
from jax import lax
from jax.sharding import PartitionSpec as P

D = 8192
BLK = 256


def gelu_parts(preact):
    inner_coef = 0.7978845608028654
    cubic_coef = 0.044715
    inner_arg = inner_coef * (preact + cubic_coef * preact * preact * preact)
    tanh_val = jnp.tanh(inner_arg)
    active = 0.5 * preact * (1.0 + tanh_val)
    slopes = 0.5 * (1.0 + tanh_val) + 0.5 * preact * (1.0 - tanh_val * tanh_val) * inner_coef * (
        1.0 + 3.0 * cubic_coef * preact * preact
    )
    return (active, slopes)


def dot_rows(left_arr, right_arr):
    return lax.dot_general(
        left_arr, right_arr, (((0,), (0,)), ((), ())), preferred_element_type=jnp.float32
    )


def dot_cols(left_arr, right_arr):
    return lax.dot_general(
        left_arr, right_arr, (((1,), (1,)), ((), ())), preferred_element_type=jnp.float32
    )


def rank_sum(values):
    return lax.psum(values, "hid")


def own_lists(lists, hid_blocks):
    return lax.dynamic_slice_in_dim(lists, lax.axis_index("hid") * hid_blocks, hid_blocks, 0)


def gather_in(values, lists, hid_blocks, blk_width):
    whole = lax.all_gather(values, "hid", axis=1, tiled=True)
    mine = own_lists(lists, hid_blocks)
    blocks = whole.reshape(whole.shape[0], whole.shape[1] // blk_width, blk_width)
    return blocks[:, mine.T]


def scatter_out(parts, lists, hid_blocks):
    mine = own_lists(lists, hid_blocks)
    picker = (mine.T[:, :, None] == jnp.arange(D // BLK, dtype=jnp.int32)[None, None, :]).astype(
        jnp.float32
    )
    dense = jnp.einsum("nsho,shc->nco", parts, picker, precision=lax.Precision.HIGHEST)
    return lax.psum_scatter(
        dense.reshape(dense.shape[0], -1), "hid", scatter_dimension=1, tiled=True
    )


def route_in(values, lists, hid_blocks, blk_width):
    return gather_in(values, lists, hid_blocks, blk_width)


def route_out(parts, lists, hid_blocks):
    return scatter_out(parts, lists, hid_blocks)


def local(
    tokens,
    in_blocks,
    in_left,
    in_right,
    in_lists,
    out_blocks,
    out_left,
    out_right,
    out_lists,
    cotangent,
):
    row_count, col_span = tokens.shape
    hid_blocks = in_blocks.shape[0]
    slot_count = in_blocks.shape[1]
    blk_width = in_blocks.shape[3]
    tok_count = lax.axis_size("tok")
    w_first, w_second, left_one, right_one, left_two, right_two = (
        lax.all_gather(in_blocks, "tok", axis=2, tiled=True),
        lax.all_gather(out_blocks, "tok", axis=2, tiled=True),
        lax.all_gather(in_left, "tok", axis=0, tiled=True),
        lax.all_gather(in_right, "tok", axis=1, tiled=True),
        lax.all_gather(out_left, "tok", axis=0, tiled=True),
        lax.all_gather(out_right, "tok", axis=1, tiled=True),
    )
    low_in, low_back = rank_sum(
        (
            jnp.dot(tokens, left_one, preferred_element_type=jnp.float32),
            dot_cols(cotangent, right_two),
        )
    )
    low_in = low_in.astype(jnp.bfloat16)
    low_back = low_back.astype(jnp.bfloat16)
    gathered = route_in(tokens, in_lists, hid_blocks, blk_width)
    group_count = gathered.shape[2]
    per_group = hid_blocks // group_count
    first_r = w_first.reshape(group_count, per_group, slot_count, blk_width, blk_width)
    second_r = w_second.reshape(group_count, per_group, slot_count, blk_width, blk_width)
    preact = jnp.einsum(
        "nseb,eqsbf->neqf", gathered, first_r, preferred_element_type=jnp.float32
    ).reshape(row_count, -1)
    preact = preact + jnp.dot(low_in, right_one, preferred_element_type=jnp.float32)
    active, slopes = gelu_parts(preact)
    hidden = active.astype(jnp.bfloat16)
    low_mid = rank_sum(jnp.dot(hidden, left_two, preferred_element_type=jnp.float32)).astype(
        jnp.bfloat16
    )
    hidden_r = hidden.reshape(row_count, group_count, per_group, blk_width)
    out_parts = jnp.einsum(
        "neqf,eqsfo->nseo", hidden_r, second_r, preferred_element_type=jnp.float32
    )
    sparse_out = route_out(out_parts, out_lists, hid_blocks)
    layer_out = (
        sparse_out + jnp.dot(low_mid, right_two, preferred_element_type=jnp.float32)
    ).astype(jnp.bfloat16)
    grad_in = route_in(cotangent, out_lists, hid_blocks, blk_width)
    grad_hidden = jnp.einsum(
        "nseo,eqsfo->neqf", grad_in, second_r, preferred_element_type=jnp.float32
    ).reshape(row_count, -1)
    grad_hidden = grad_hidden + dot_cols(low_back, left_two)
    grad_pre = (grad_hidden * slopes).astype(jnp.bfloat16)
    low_grad = rank_sum(dot_cols(grad_pre, right_one)).astype(jnp.bfloat16)
    grad_pre_r = grad_pre.reshape(row_count, group_count, per_group, blk_width)
    back_parts = jnp.einsum(
        "neqf,eqsbf->nseb", grad_pre_r, first_r, preferred_element_type=jnp.float32
    )
    sparse_back = route_out(back_parts, in_lists, hid_blocks)
    grad_tokens = (sparse_back + dot_cols(low_grad, left_one)).astype(jnp.bfloat16)
    loss_scale = lax.rsqrt(jnp.float32(row_count * tok_count))
    terms = (
        loss_scale
        * jnp.einsum(
            "nseb,neqf->eqsbf", gathered, grad_pre_r, preferred_element_type=jnp.float32
        ).reshape(w_first.shape),
        loss_scale
        * jnp.einsum(
            "neqf,nseo->eqsfo", hidden_r, grad_in, preferred_element_type=jnp.float32
        ).reshape(w_second.shape),
        loss_scale * dot_rows(tokens, low_grad),
        loss_scale * dot_rows(low_in, grad_pre),
        loss_scale * dot_rows(hidden, low_back),
        loss_scale * dot_rows(low_mid, cotangent),
    )
    shares = (
        lax.psum_scatter(
            terms[0].astype(jnp.bfloat16), "tok", scatter_dimension=2, tiled=True
        ).astype(jnp.float32),
        lax.psum_scatter(
            terms[1].astype(jnp.bfloat16), "tok", scatter_dimension=2, tiled=True
        ).astype(jnp.float32),
        lax.psum_scatter(
            terms[2].astype(jnp.bfloat16), "tok", scatter_dimension=0, tiled=True
        ).astype(jnp.float32),
        lax.psum_scatter(
            terms[3].astype(jnp.bfloat16), "tok", scatter_dimension=1, tiled=True
        ).astype(jnp.float32),
        lax.psum_scatter(
            terms[4].astype(jnp.bfloat16), "tok", scatter_dimension=0, tiled=True
        ).astype(jnp.float32),
        lax.psum_scatter(
            terms[5].astype(jnp.bfloat16), "tok", scatter_dimension=1, tiled=True
        ).astype(jnp.float32),
    )
    return (
        layer_out,
        grad_tokens,
        shares[0].astype(jnp.bfloat16),
        shares[2].astype(jnp.bfloat16),
        shares[3].astype(jnp.bfloat16),
        shares[1].astype(jnp.bfloat16),
        shares[4].astype(jnp.bfloat16),
        shares[5].astype(jnp.bfloat16),
    )


def solution(mesh):
    return jax.shard_map(
        local,
        mesh=mesh,
        in_specs=(
            P("tok", "hid"),
            P("hid", None, "tok", None),
            P(("hid", "tok"), None),
            P(None, ("hid", "tok")),
            P(),
            P("hid", None, "tok", None),
            P(("hid", "tok"), None),
            P(None, ("hid", "tok")),
            P(),
            P("tok", "hid"),
        ),
        out_specs=(
            P("tok", "hid"),
            P("tok", "hid"),
            P("hid", None, "tok", None),
            P(("hid", "tok"), None),
            P(None, ("hid", "tok")),
            P("hid", None, "tok", None),
            P(("hid", "tok"), None),
            P(None, ("hid", "tok")),
        ),
        check_vma=False,
    )
```

profile of v0, /device:TPU:0, one launch (start us, length us, event | category | flops | bytes accessed | tf_op | source)
XLA Modules:
  0.0 1396.9 jit_solution(3682937672715421164)
XLA Ops:
  13.0 17.4 %all_gather.26 = bf16[1024,256]{1,0:T(8,128)(2,1)S(1)} all-gather(bf16[256,256]{1,0:T(8,128)(2,1)S(1)} %copy-done.12), channel_id=1, replica_groups=mesh['hid'=8,'tok'=4] {'tok'}, dimensions={0}, use_global_device_ids=true | all-gather | bytes 655360 | tf_op jit(solution)/shard_map/all_gather | solution.py:88
  31.5 16.3 %all_gather.30 = bf16[256,1024]{1,0:T(8,128)(2,1)S(1)} all-gather(bf16[256,256]{1,0:T(8,128)(2,1)S(1)} %copy-done.13), channel_id=1, replica_groups=mesh['hid'=8,'tok'=4] {'tok'}, dimensions={1}, use_global_device_ids=true | all-gather | bytes 655360 | tf_op jit(solution)/shard_map/all_gather | solution.py:91
  48.9 32.9 %all-reduce.4 = (bf16[224,256]{1,0:T(8,128)(2,1)S(1)}, bf16[224,256]{1,0:T(8,128)(2,1)S(1)}) all-reduce(f32[224,256]{1,0:T(8,128)S(1)} %fusion.60, f32[224,256]{1,0:T(8,128)S(1)} %fusion.62), channel_id=1, replica_groups=mesh['hid'=8,'tok'=4] {'hid'}, use_global_device_ids=true, to_apply=%region_0.0 | all-reduce | flops 114688 | bytes 688128 | tf_op jit(solution)/shard_map/psum | solution.py:35
  90.8 11.0 gather_fusion.1
  101.8 10.5 gather_fusion
  112.3 194.0 %all-gather.13.cloned.1.call-done = bf16[16,6,256,256]{3,2,1,0:T(8,128)(2,1)} async-done(((bf16[16,6,64,256]{3,2,1,0:T(8,128)(2,1)}), bf16[16,6,256,256]{3,2,1,0:T(8,128)(2,1)}) %all-gather.13.cloned.1.call-update) | async-done | bytes 12582928 | tf_op jit(solution)/shard_map/all_gather | solution.py:87
  306.3 10.4 fusion.57
  318.8 205.9 %all-gather.9.cloned.1.call-done = bf16[16,6,256,256]{3,2,0,1:T(8,128)(2,1)} async-done(((bf16[16,6,64,256]{3,2,0,1:T(8,128)(2,1)}), bf16[16,6,256,256]{3,2,0,1:T(8,128)(2,1)}) %all-gather.9.cloned.1.call-update) | async-done | bytes 12582928 | tf_op jit(solution)/shard_map/all_gather | solution.py:86
  524.7 12.0 fusion.56
  539.1 31.2 %all-gather.11.cloned.1.call-done = bf16[256,4096]{1,0:T(8,128)(2,1)} async-done(((bf16[256,1024]{1,0:T(8,128)(2,1)}), bf16[256,4096]{1,0:T(8,128)(2,1)}) %all-gather.11.cloned.1.call-update) | async-done | bytes 2097168 | tf_op jit(solution)/shard_map/all_gather | solution.py:89
  570.3 6.7 multiply_convert_fusion.2
  577.0 39.4 %all-gather.15.cloned.1.call-done = bf16[4096,256]{1,0:T(8,128)(2,1)} async-done(((bf16[1024,256]{1,0:T(8,128)(2,1)}), bf16[4096,256]{1,0:T(8,128)(2,1)}) %all-gather.15.cloned.1.call-update) | async-done | bytes 2097168 | tf_op jit(solution)/shard_map/all_gather | solution.py:90
  616.4 6.0 fusion.24
  625.2 29.4 %all-reduce.5 = (bf16[224,256]{1,0:T(8,128)(2,1)S(1)}, bf16[224,256]{1,0:T(8,128)(2,1)S(1)}) all-reduce(f32[224,256]{1,0:T(8,128)S(1)} %fusion.61, f32[224,256]{1,0:T(8,128)S(1)} %fusion.63), channel_id=1, replica_groups=mesh['hid'=8,'tok'=4] {'hid'}, use_global_device_ids=true, to_apply=%region_2.0 | all-reduce | flops 114688 | bytes 688128 | tf_op jit(solution)/shard_map/psum | solution.py:35
  657.6 13.2 fusion.14
  670.8 28.7 %fusion = f32[32,224,256,1]{2,0,3,1:T(8,128)S(1)} fusion(f32[224,6,16,256]{3,0,1,2:T(8,128)} %fusion.14, s32[6,16]{1,0:T(8,128)S(1)} %get-tuple-element.47), kind=kOutput, calls=%fused_computation.4 | convolution fusion | flops 2113932288 | bytes 29360512 | tf_op jit(solution)/shard_map/nsho,shc->nco/dot_general | solution.py:54
  699.5 9.4 copy.94
  711.0 16.4 %convolution_bitcast_fusion = f32[224,6,16,256]{3,0,1,2:T(8,128)} fusion(bf16[16,6,256,256]{3,2,1,0:T(8,128)(2,1)} %all-gather.13.cloned.1.call-done, bf16[224,16,256,1]{2,1,0,3:T(8,128)(2,1)S(1)} %bitcast.141), kind=kOutput, calls=%fused_computation.19 | convolution fusion | flops 2818572288 | bytes 36438016 | tf_op jit(solution)/shard_map/neqf,eqsfo->nseo/dot_general | solution.py:116
  727.4 28.5 %fusion.2 = f32[32,224,256,1]{2,0,3,1:T(8,128)S(1)} fusion(f32[224,6,16,256]{3,0,1,2:T(8,128)} %convolution_bitcast_fusion, s32[6,16]{1,0:T(8,128)S(1)} %get-tuple-element.45), kind=kOutput, calls=%fused_computation.6 | convolution fusion | flops 2113932288 | bytes 29360512 | tf_op jit(solution)/shard_map/nsho,shc->nco/dot_general | solution.py:54
  755.9 9.5 copy.91
  765.5 11.5 fusion.5
  777.0 17.2 %copy.69 = bf16[16,6,256,256]{3,0,1,2:T(8,128)(2,1)} copy(bf16[16,6,256,256]{2,3,1,0:T(8,128)(2,1)} %fusion.5) | data formatting | bytes 25165824 | tf_op jit(solution)/shard_map/convert_element_type | solution.py:156
  794.2 12.0 fusion.4
  806.3 17.0 %copy.66 = bf16[16,6,256,256]{3,0,1,2:T(8,128)(2,1)} copy(bf16[16,6,256,256]{2,3,1,0:T(8,128)(2,1)} %fusion.4) | data formatting | bytes 25165824 | tf_op jit(solution)/shard_map/convert_element_type | solution.py:153
  835.2 8.8 reduce-scatter.9.cloned.1.call-done
  846.3 211.8 %reduce-scatter.19.cloned.1.call-done = bf16[16,6,64,256]{3,0,1,2:T(8,128)(2,1)} async-done(((bf16[16,6,256,256]{3,0,1,2:T(8,128)(2,1)}), bf16[16,6,64,256]{3,0,1,2:T(8,128)(2,1)}) %reduce-scatter.19.cloned.1.call-update) | async-done | bytes 3145744 | tf_op jit(solution)/shard_map/reduce_scatter | solution.py:155
  1058.2 5.3 copy.72
  1063.5 209.9 %reduce-scatter.13.cloned.1.call-done = bf16[16,6,64,256]{3,0,1,2:T(8,128)(2,1)} async-done(((bf16[16,6,256,256]{3,0,1,2:T(8,128)(2,1)}), bf16[16,6,64,256]{3,0,1,2:T(8,128)(2,1)}) %reduce-scatter.13.cloned.1.call-update) | async-done | bytes 3145744 | tf_op jit(solution)/shard_map/reduce_scatter | solution.py:152
  1273.4 5.3 copy.70
  1278.8 20.1 %reduce-scatter.23.cloned.1.call-done = bf16[256,256]{1,0:T(8,128)(2,1)} async-done(((bf16[256,1024]{1,0:T(8,128)(2,1)}), bf16[256,256]{1,0:T(8,128)(2,1)}) %reduce-scatter.23.cloned.1.call-update) | async-done | bytes 131088 | tf_op jit(solution)/shard_map/reduce_scatter | solution.py:167
  1298.9 45.0 %reduce-scatter.21.cloned.1.call-done = bf16[1024,256]{1,0:T(8,128)(2,1)} async-done(((bf16[4096,256]{1,0:T(8,128)(2,1)}), bf16[1024,256]{1,0:T(8,128)(2,1)}) %reduce-scatter.21.cloned.1.call-update) | async-done | bytes 524304 | tf_op jit(solution)/shard_map/reduce_scatter | solution.py:164
  1343.9 46.0 %reduce-scatter.17.cloned.1.call-done = bf16[256,1024]{1,0:T(8,128)(2,1)} async-done(((bf16[256,4096]{1,0:T(8,128)(2,1)}), bf16[256,1024]{1,0:T(8,128)(2,1)}) %reduce-scatter.17.cloned.1.call-update) | async-done | bytes 524304 | tf_op jit(solution)/shard_map/reduce_scatter | solution.py:161
  (88 shorter events, 43.5 us)
Async XLA Ops:
  7.2 2.3 copy-start.10
  7.2 74.7 %all-gather.7.cloned.1.call-start = ((), (), s32[]{:S(2)}) async-start(), calls=%async_computation.8 | async-start | bytes 4128768 | tf_op jit(solution)/shard_map/all_gather | solution.py:43
  7.9 78.6 %all-gather.17.cloned.1.call-start = ((), (), s32[]{:S(2)}) async-start(), calls=%async_computation.14 | async-start | bytes 4128768 | tf_op jit(solution)/shard_map/all_gather | solution.py:43
  8.7 297.6 %all-gather.13.cloned.1.call-start = ((), (), s32[]{:S(2)}) async-start(), calls=%async_computation.11 | async-start | bytes 15728640 | tf_op jit(solution)/shard_map/all_gather | solution.py:87
  9.4 515.3 %all-gather.9.cloned.1.call-start = ((), (), s32[]{:S(2)}) async-start(), calls=%async_computation.9 | async-start | bytes 15728640 | tf_op jit(solution)/shard_map/all_gather | solution.py:86
  11.3 1.3 copy-start.14
  11.3 1.5 copy-start.15
  11.3 1.6 copy-start.12
  11.3 19.8 %copy-start.7 = (bf16[224,1024]{1,0:T(8,128)(2,1)S(1)}, bf16[224,1024]{1,0:T(8,128)(2,1)}, u32[]{:S(2)}) copy-start(bf16[224,1024]{1,0:T(8,128)(2,1)} %param.10) | copy-start | bytes 1376260
  11.3 20.1 %copy-start.13 = (bf16[256,256]{1,0:T(8,128)(2,1)S(1)}, bf16[256,256]{1,0:T(8,128)(2,1)}, u32[]{:S(2)}) copy-start(bf16[256,256]{1,0:T(8,128)(2,1)} %param.17) | copy-start | bytes 393220
  11.4 37.2 %copy-start.8 = (bf16[224,1024]{1,0:T(8,128)(2,1)S(1)}, bf16[224,1024]{1,0:T(8,128)(2,1)}, u32[]{:S(2)}) copy-start(bf16[224,1024]{1,0:T(8,128)(2,1)} %param.19) | copy-start | bytes 1376260
  11.4 558.9 %all-gather.11.cloned.1.call-start = ((), (), s32[]{:S(2)}) async-start(), calls=%async_computation.10 | async-start | bytes 2621440 | tf_op jit(solution)/shard_map/all_gather | solution.py:89
  12.0 604.4 %all-gather.15.cloned.1.call-start = ((), (), s32[]{:S(2)}) async-start(), calls=%async_computation.13 | async-start | bytes 2621440 | tf_op jit(solution)/shard_map/all_gather | solution.py:90
  12.6 818.7 %reduce-scatter.15.cloned.1.call-start = ((), (), s32[]{:S(2)}) async-start(), calls=%async_computation.17 | async-start | bytes 655360 | tf_op jit(solution)/shard_map/reduce_scatter | solution.py:158
  30.3 0.8 copy-start.5
  47.7 0.8 copy-start.3
  616.4 6.0 copy-start.2
  622.4 1.5 copy-start
  622.4 2.1 copy-start.11
  655.8 177.1 %reduce-scatter.11.cloned.1.call-start = ((), (), s32[]{:S(2)}) async-start(), calls=%async_computation.15 | async-start | bytes 8257536 | tf_op jit(solution)/shard_map/reduce_scatter | solution.py:55
  709.0 135.1 %reduce-scatter.9.cloned.1.call-start = ((), (), s32[]{:S(2)}) async-start(), calls=%async_computation.12 | async-start | bytes 8257536 | tf_op jit(solution)/shard_map/reduce_scatter | solution.py:55
  711.0 16.4 %copy-start.1 = (bf16[28,8,16,256]{3,2,1,0:T(8,128)(2,1)}, bf16[28,8,16,256]{3,2,1,0:T(8,128)(2,1)S(1)}, u32[]{:S(2)}) copy-start(bf16[28,8,16,256]{3,2,1,0:T(8,128)(2,1)S(1)} %copy.90) | copy-start | bytes 5505028
  765.5 292.7 %reduce-scatter.19.cloned.1.call-start = ((), (), s32[]{:S(2)}) async-start(), calls=%async_computation.19 | async-start | bytes 15728640 | tf_op jit(solution)/shard_map/reduce_scatter | solution.py:155
  794.2 479.3 %reduce-scatter.13.cloned.1.call-start = ((), (), s32[]{:S(2)}) async-start(), calls=%async_computation.16 | async-start | bytes 15728640 | tf_op jit(solution)/shard_map/reduce_scatter | solution.py:152
  823.3 1.0 copy-start.9
  823.3 475.6 %reduce-scatter.23.cloned.1.call-start = ((), (), s32[]{:S(2)}) async-start(), calls=%async_computation.21 | async-start | bytes 655360 | tf_op jit(solution)/shard_map/reduce_scatter | solution.py:167
  825.4 518.5 %reduce-scatter.21.cloned.1.call-start = ((), (), s32[]{:S(2)}) async-start(), calls=%async_computation.20 | async-start | bytes 2621440 | tf_op jit(solution)/shard_map/reduce_scatter | solution.py:164
  829.1 3.8 copy-start.6
  829.1 15.0 %copy-start.4 = (bf16[256,1024]{1,0:T(8,128)(2,1)S(1)}, bf16[256,1024]{1,0:T(8,128)(2,1)}, u32[]{:S(2)}) copy-start(bf16[256,1024]{1,0:T(8,128)(2,1)} %copy-done.3) | copy-start | bytes 1572868
  829.1 560.8 %reduce-scatter.17.cloned.1.call-start = ((), (), s32[]{:S(2)}) async-start(), calls=%async_computation.18 | async-start | bytes 2621440 | tf_op jit(solution)/shard_map/reduce_scatter | solution.py:161
Sparse Core Ops, SparseCore 0:
  9.9 37.2 all-gather.6
  49.1 37.3 all-gather.16
  88.0 218.1 all-gather.12
  308.3 216.3 all-gather.8
  526.1 44.1 all-gather.10
  571.7 44.6 all-gather.14
  656.0 19.1 reduce-scatter.14
  709.1 64.2 reduce-scatter.10
  777.1 66.9 reduce-scatter.8
  846.3 211.8 reduce-scatter.18
  1060.5 212.8 reduce-scatter.12
  1276.1 22.6 reduce-scatter.22
  1301.7 42.1 reduce-scatter.20
  1346.7 43.1 reduce-scatter.16
where the time goes:
time: 1410 us; the launch traced here: 1400 us
  waiting for transfers between devices  1020 us (72%)
  matrix products  160 us (11%)
  local copies, waits for them, and re-layouts  110 us (8%)
  blocking collectives  96 us (7%)
  between operations  14.6 us (1%)
    reduce_scatter x1, waiting for transfers between devices, local(): lax.psum_scatter(terms[1].astype(jnp.bfloat16), 'tok', scatter_dimension=...  212 us
    reduce_scatter x1, waiting for transfers between devices, local(): lax.psum_scatter(terms[0].astype(jnp.bfloat16), 'tok', scatter_dimension=...  210 us
    all_gather x1, waiting for transfers between devices, local(): lax.all_gather(in_blocks, 'tok', axis=2, tiled=True)  206 us
    all_gather x1, waiting for transfers between devices, local(): lax.all_gather(out_blocks, 'tok', axis=2, tiled=True)  194 us
    psum x2, blocking collectives, rank_sum(): return lax.psum(values, 'hid')  62.3 us
    dot_general x2, matrix products, scatter_out(): jnp.einsum('nsho,shc->nco', parts, picker, precision=lax.Precision.HIGHEST)  57.2 us
    reduce_scatter x1, waiting for transfers between devices, local(): lax.psum_scatter(terms[3].astype(jnp.bfloat16), 'tok', scatter_dimension=...  46 us
    unnamed x42, local copies, waits for them, and re-layouts  45.3 us
  transfers between devices with their start and end apart: 14, of which 11 were waited for; matrix products, arithmetic and copies ran while one was open for 18% of the time, Pallas kernels for 0%

commit v1 on v0

--- a/solution.py
+++ b/solution.py
@@ -5,6 +5,22 @@
 
 D = 8192
 BLK = 256
+
+
+def gather_around(x, axis, dim):
+    ways, here, step = (lax.axis_size(axis), lax.axis_index(axis), x.shape[dim])
+    lengths = [n * ways if d == dim else n for d, n in enumerate(x.shape)]
+    full = lax.dynamic_update_slice_in_dim(jnp.zeros(lengths, x.dtype), x, here * step, axis=dim)
+    going_up = going_down = x
+    for far in range(1, ways // 2 + 1):
+        going_up = lax.ppermute(going_up, axis, [(d, (d + 1) % ways) for d in range(ways)])
+        full = lax.dynamic_update_slice_in_dim(full, going_up, (here - far) % ways * step, axis=dim)
+        if 2 * far < ways:
+            going_down = lax.ppermute(going_down, axis, [(d, (d - 1) % ways) for d in range(ways)])
+            full = lax.dynamic_update_slice_in_dim(
+                full, going_down, (here + far) % ways * step, axis=dim
+            )
+    return full
 
 
 def gelu_parts(preact):
@@ -83,7 +99,7 @@
     blk_width = in_blocks.shape[3]
     tok_count = lax.axis_size("tok")
     w_first, w_second, left_one, right_one, left_two, right_two = (
-        lax.all_gather(in_blocks, "tok", axis=2, tiled=True),
+        gather_around(in_blocks, "tok", 2),
         lax.all_gather(out_blocks, "tok", axis=2, tiled=True),
         lax.all_gather(in_left, "tok", axis=0, tiled=True),
         lax.all_gather(in_right, "tok", axis=1, tiled=True),

time: 1410 us -> 1310 us (0.929)
  waiting for transfers between devices: 1020 us -> 701 us
  blocking collectives: 96 us -> 263 us
  starting transfers between devices: 0.56 us -> 30.7 us
  local copies, waits for them, and re-layouts: 110 us -> 126 us
    all_gather x1 -> x0, waiting for transfers between devices: 206 us -> none  [local(): lax.all_gather(in_blocks, 'tok', axis=2, tiled=True)]
    all_gather x1, blocking collectives: 17.4 us -> 177 us  [local(): lax.all_gather(in_left, 'tok', axis=0, tiled=True)]
    all_gather x1, waiting for transfers between devices: 194 us -> 60.4 us  [local(): lax.all_gather(out_blocks, 'tok', axis=2, tiled=True)]
    ppermute x0 -> x3, waiting for transfers between devices: none -> 93 us  [the longest x2 93 us: gather_around(): lax.ppermute(going_up, axis, [(d, (d + 1) % ways) for d in range(ways)])]
    all_gather x1, waiting for transfers between devices: 39.4 us -> 0.01 us  [local(): lax.all_gather(out_left, 'tok', axis=0, tiled=True)]
    all_gather x1, waiting for transfers between devices: 31.2 us -> 0.01 us  [local(): lax.all_gather(in_right, 'tok', axis=1, tiled=True)]
    ppermute x0 -> x3, starting transfers between devices: none -> 30.2 us  [the longest x2 28.1 us: gather_around(): lax.ppermute(going_up, axis, [(d, (d + 1) % ways) for d in range(ways)])]
    unnamed x42 -> x41, local copies, waits for them, and re-layouts: 45.3 us -> 43.4 us
  transfers between devices with their start and end apart: 14 -> 16, of which waited for: 11 -> 8; matrix products, arithmetic and copies ran while one was open for 18% -> 21% of each run, Pallas kernels for 0% -> 0%
where the time goes in v1:
time: 1310 us; the launch traced here: 1300 us
  waiting for transfers between devices  701 us (54%)
  blocking collectives  263 us (20%)
  matrix products  161 us (12%)
  local copies, waits for them, and re-layouts  126 us (10%)
  starting transfers between devices  30.7 us (2%)
  between operations  14.6 us (1%)
    reduce_scatter x1, waiting for transfers between devices, local(): lax.psum_scatter(terms[1].astype(jnp.bfloat16), 'tok', scatter_dimension=...  212 us
    reduce_scatter x1, waiting for transfers between devices, local(): lax.psum_scatter(terms[0].astype(jnp.bfloat16), 'tok', scatter_dimension=...  210 us
    all_gather x1, blocking collectives, local(): lax.all_gather(in_left, 'tok', axis=0, tiled=True)  177 us
    ppermute x2, waiting for transfers between devices, gather_around(): lax.ppermute(going_up, axis, [(d, (d + 1) % ways) for d in range(ways)])  93 us
    all_gather x1, waiting for transfers between devices, local(): lax.all_gather(out_blocks, 'tok', axis=2, tiled=True)  60.4 us
    psum x2, blocking collectives, rank_sum(): return lax.psum(values, 'hid')  59.5 us
    dot_general x2, matrix products, scatter_out(): jnp.einsum('nsho,shc->nco', parts, picker, precision=lax.Precision.HIGHEST)  57.6 us
    reduce_scatter x1, waiting for transfers between devices, local(): lax.psum_scatter(terms[3].astype(jnp.bfloat16), 'tok', scatter_dimension=...  45.1 us
  transfers between devices with their start and end apart: 16, of which 8 were waited for; matrix products, arithmetic and copies ran while one was open for 21% of the time, Pallas kernels for 0%

profile of v1, /device:TPU:0, one launch (start us, length us, event | category | flops | bytes accessed | tf_op | source)
XLA Modules:
  0.0 1296.4 jit_solution(5500704883681599650)
XLA Ops:
  15.8 93.0 %collective-permute-done = bf16[16,6,64,256]{3,2,1,0:T(8,128)(2,1)} collective-permute-done((bf16[16,6,64,256]{3,2,1,0:T(8,128)(2,1)}, bf16[16,6,64,256]{3,2,1,0:T(8,128)(2,1)}, u32[]{:S(2)}, u32[]{:S(2)}) %collective-permute-start) | collective-permute-done | bytes 3145760 | tf_op jit(solution)/shard_map/ppermute | solution.py:16
  108.8 25.0 %collective-permute-start.2 = (bf16[16,6,64,256]{3,2,1,0:T(8,128)(2,1)}, bf16[16,6,64,256]{3,2,1,0:T(8,128)(2,1)}, u32[]{:S(2)}, u32[]{:S(2)}) collective-permute-start(bf16[16,6,64,256]{3,2,1,0:T(8,128)(2,1)} %collective-permute-done), channel_id=1, source_target_pairs={{0,1},{1,2},{2,3},{3,0},{4,5},{5,6},{6,7},{7,4},{8,9},{9,10},{10,1... | collective-permute-start | bytes 9437192 | tf_op jit(solution)/shard_map/ppermute | solution.py:16
  134.0 176.6 %all_gather.22 = bf16[1024,256]{1,0:T(8,128)(2,1)S(1)} all-gather(bf16[256,256]{1,0:T(8,128)(2,1)S(1)} %copy-done.12), channel_id=1, replica_groups=mesh['hid'=8,'tok'=4] {'tok'}, dimensions={0}, use_global_device_ids=true | all-gather | bytes 655360 | tf_op jit(solution)/shard_map/all_gather | solution.py:104
  311.7 27.1 %all_gather.26 = bf16[256,1024]{1,0:T(8,128)(2,1)S(1)} all-gather(bf16[256,256]{1,0:T(8,128)(2,1)S(1)} %copy-done.13), channel_id=1, replica_groups=mesh['hid'=8,'tok'=4] {'tok'}, dimensions={1}, use_global_device_ids=true | all-gather | bytes 655360 | tf_op jit(solution)/shard_map/all_gather | solution.py:107
  340.1 29.4 %all-reduce.4 = (bf16[224,256]{1,0:T(8,128)(2,1)S(1)}, bf16[224,256]{1,0:T(8,128)(2,1)S(1)}) all-reduce(f32[224,256]{1,0:T(8,128)S(1)} %fusion.62, f32[224,256]{1,0:T(8,128)S(1)} %fusion.64), channel_id=1, replica_groups=mesh['hid'=8,'tok'=4] {'hid'}, use_global_device_ids=true, to_apply=%region_0.1 | all-reduce | flops 114688 | bytes 688128 | tf_op jit(solution)/shard_map/psum | solution.py:51
  369.6 6.1 broadcast.44
  389.4 4.4 copy.131
  393.8 10.1 gather_fusion
  403.9 12.8 fusion.59
  421.0 6.1 multiply_convert_fusion.2
  435.5 10.2 gather_fusion.1
  445.7 60.4 %all-gather.10.cloned.1.call-done = bf16[16,6,256,256]{3,2,1,0:T(8,128)(2,1)} async-done(((bf16[16,6,64,256]{3,2,1,0:T(8,128)(2,1)}), bf16[16,6,256,256]{3,2,1,0:T(8,128)(2,1)}) %all-gather.10.cloned.1.call-update) | async-done | bytes 12582928 | tf_op jit(solution)/shard_map/all_gather | solution.py:103
  506.1 10.0 fusion.56
  522.6 30.0 %all-reduce.5 = (bf16[224,256]{1,0:T(8,128)(2,1)S(1)}, bf16[224,256]{1,0:T(8,128)(2,1)S(1)}) all-reduce(f32[224,256]{1,0:T(8,128)S(1)} %fusion.63, f32[224,256]{1,0:T(8,128)S(1)} %fusion.65), channel_id=1, replica_groups=mesh['hid'=8,'tok'=4] {'hid'}, use_global_device_ids=true, to_apply=%region_2.3 | all-reduce | flops 114688 | bytes 688128 | tf_op jit(solution)/shard_map/psum | solution.py:51
  553.9 16.0 %convolution_bitcast_fusion.1 = f32[224,6,16,256]{3,0,1,2:T(8,128)} fusion(bf16[16,6,256,256]{3,2,1,0:T(8,128)(2,1)} %all-gather.10.cloned.1.call-done, bf16[224,16,256,1]{2,1,0,3:T(8,128)(2,1)} %bitcast.139), kind=kOutput, calls=%fused_computation.19 | convolution fusion | flops 2818572288 | bytes 36438016 | tf_op jit(solution)/shard_map/neqf,eqsfo->nseo/dot_general | solution.py:132
  569.9 29.1 %fusion.2 = f32[32,224,256,1]{2,0,3,1:T(8,128)S(1)} fusion(f32[224,6,16,256]{3,0,1,2:T(8,128)} %convolution_bitcast_fusion.1, s32[6,16]{1,0:T(8,128)S(1)} %get-tuple-element.45), kind=kOutput, calls=%fused_computation.6 | convolution fusion | flops 2113932288 | bytes 29360512 | tf_op jit(solution)/shard_map/nsho,shc->nco/dot_general | solution.py:70
  598.9 9.5 copy.90
  610.2 15.1 %convolution_bitcast_fusion = f32[224,6,16,256]{3,0,1,2:T(8,128)} fusion(bf16[16,6,256,256]{3,2,1,0:T(8,128)(2,1)} %constant_dynamic-update-slice_fusion, bf16[224,16,256,1]{2,1,0,3:T(8,128)(2,1)} %bitcast.137), kind=kOutput, calls=%fused_computation.18 | convolution fusion | flops 2818572288 | bytes 36438016 | tf_op jit(solution)/shard_map/neqf,eqsbf->nseb/dot_general | solution.py:147
  625.3 28.5 %fusion = f32[32,224,256,1]{2,0,3,1:T(8,128)S(1)} fusion(f32[224,6,16,256]{3,0,1,2:T(8,128)} %convolution_bitcast_fusion, s32[6,16]{1,0:T(8,128)S(1)} %get-tuple-element.47), kind=kOutput, calls=%fused_computation.4 | convolution fusion | flops 2113932288 | bytes 29360512 | tf_op jit(solution)/shard_map/nsho,shc->nco/dot_general | solution.py:70
  653.8 9.4 copy.93
  663.3 11.5 fusion.5
  674.8 17.3 %copy.67 = bf16[16,6,256,256]{3,0,1,2:T(8,128)(2,1)} copy(bf16[16,6,256,256]{2,3,1,0:T(8,128)(2,1)} %fusion.5) | data formatting | bytes 25165824 | tf_op jit(solution)/shard_map/convert_element_type | solution.py:172
  692.2 12.2 fusion.4
  704.4 16.4 %copy.64 = bf16[16,6,256,256]{3,0,1,2:T(8,128)(2,1)} copy(bf16[16,6,256,256]{2,3,1,0:T(8,128)(2,1)} %fusion.4) | data formatting | bytes 25165824 | tf_op jit(solution)/shard_map/convert_element_type | solution.py:169
  732.2 11.3 reduce-scatter.11.cloned.1.call-done
  745.7 212.0 %reduce-scatter.19.cloned.1.call-done = bf16[16,6,64,256]{3,0,1,2:T(8,128)(2,1)} async-done(((bf16[16,6,256,256]{3,0,1,2:T(8,128)(2,1)}), bf16[16,6,64,256]{3,0,1,2:T(8,128)(2,1)}) %reduce-scatter.19.cloned.1.call-update) | async-done | bytes 3145744 | tf_op jit(solution)/shard_map/reduce_scatter | solution.py:171
  957.7 5.3 copy.70
  963.0 209.8 %reduce-scatter.13.cloned.1.call-done = bf16[16,6,64,256]{3,0,1,2:T(8,128)(2,1)} async-done(((bf16[16,6,256,256]{3,0,1,2:T(8,128)(2,1)}), bf16[16,6,64,256]{3,0,1,2:T(8,128)(2,1)}) %reduce-scatter.13.cloned.1.call-update) | async-done | bytes 3145744 | tf_op jit(solution)/shard_map/reduce_scatter | solution.py:168
  1172.8 5.3 copy.68
  1178.1 42.5 %reduce-scatter.21.cloned.1.call-done = bf16[1024,256]{1,0:T(8,128)(2,1)} async-done(((bf16[4096,256]{1,0:T(8,128)(2,1)}), bf16[1024,256]{1,0:T(8,128)(2,1)}) %reduce-scatter.21.cloned.1.call-update) | async-done | bytes 524304 | tf_op jit(solution)/shard_map/reduce_scatter | solution.py:180
  1220.6 23.8 %reduce-scatter.23.cloned.1.call-done = bf16[256,256]{1,0:T(8,128)(2,1)} async-done(((bf16[256,1024]{1,0:T(8,128)(2,1)}), bf16[256,256]{1,0:T(8,128)(2,1)}) %reduce-scatter.23.cloned.1.call-update) | async-done | bytes 131088 | tf_op jit(solution)/shard_map/reduce_scatter | solution.py:183
  1244.4 45.1 %reduce-scatter.17.cloned.1.call-done = bf16[256,1024]{1,0:T(8,128)(2,1)} async-done(((bf16[256,4096]{1,0:T(8,128)(2,1)}), bf16[256,1024]{1,0:T(8,128)(2,1)}) %reduce-scatter.17.cloned.1.call-update) | async-done | bytes 524304 | tf_op jit(solution)/shard_map/reduce_scatter | solution.py:177
  (95 shorter events, 60.6 us)
Async XLA Ops:
  7.2 304.2 %copy-start.6 = (bf16[224,1024]{1,0:T(8,128)(2,1)S(1)}, bf16[224,1024]{1,0:T(8,128)(2,1)}, u32[]{:S(2)}) copy-start(bf16[224,1024]{1,0:T(8,128)(2,1)} %param.10) | copy-start | bytes 1376260
  7.2 126.7 %copy-start.14 = (s32[128,6]{0,1:T(8,128)S(1)}, s32[128,6]{0,1:T(8,128)}, u32[]{:S(2)}) copy-start(s32[128,6]{0,1:T(8,128)} %param.14) | copy-start | bytes 9220
  7.2 126.8 %copy-start.12 = (bf16[256,256]{1,0:T(8,128)(2,1)S(1)}, bf16[256,256]{1,0:T(8,128)(2,1)}, u32[]{:S(2)}) copy-start(bf16[256,256]{1,0:T(8,128)(2,1)} %param.12) | copy-start | bytes 393220
  7.2 304.5 %copy-start.13 = (bf16[256,256]{1,0:T(8,128)(2,1)S(1)}, bf16[256,256]{1,0:T(8,128)(2,1)}, u32[]{:S(2)}) copy-start(bf16[256,256]{1,0:T(8,128)(2,1)} %param.17) | copy-start | bytes 393220
  7.2 382.2 %all-gather.6.cloned.1.call-start = ((), (), s32[]{:S(2)}) async-start(), calls=%async_computation.8 | async-start | bytes 4128768 | tf_op jit(solution)/shard_map/all_gather | solution.py:59
  7.9 331.6 %copy-start.7 = (bf16[224,1024]{1,0:T(8,128)(2,1)S(1)}, bf16[224,1024]{1,0:T(8,128)(2,1)}, u32[]{:S(2)}) copy-start(bf16[224,1024]{1,0:T(8,128)(2,1)} %param.19) | copy-start | bytes 1376260
  8.0 413.0 %all-gather.8.cloned.1.call-start = ((), (), s32[]{:S(2)}) async-start(), calls=%async_computation.9 | async-start | bytes 2621440 | tf_op jit(solution)/shard_map/all_gather | solution.py:105
  8.7 420.2 %all-gather.12.cloned.1.call-start = ((), (), s32[]{:S(2)}) async-start(), calls=%async_computation.12 | async-start | bytes 2621440 | tf_op jit(solution)/shard_map/all_gather | solution.py:106
  9.4 330.5 %copy-start.15 = (s32[128,6]{0,1:T(8,128)S(1)}, s32[128,6]{0,1:T(8,128)}, u32[]{:S(2)}) copy-start(s32[128,6]{0,1:T(8,128)} %param.18) | copy-start | bytes 9220
  9.4 421.7 %all-gather.14.cloned.1.call-start = ((), (), s32[]{:S(2)}) async-start(), calls=%async_computation.13 | async-start | bytes 4128768 | tf_op jit(solution)/shard_map/all_gather | solution.py:59
  10.0 496.1 %all-gather.10.cloned.1.call-start = ((), (), s32[]{:S(2)}) async-start(), calls=%async_computation.10 | async-start | bytes 15728640 | tf_op jit(solution)/shard_map/all_gather | solution.py:103
  10.6 717.5 %reduce-scatter.15.cloned.1.call-start = ((), (), s32[]{:S(2)}) async-start(), calls=%async_computation.16 | async-start | bytes 655360 | tf_op jit(solution)/shard_map/reduce_scatter | solution.py:174
  10.7 98.2 %collective-permute-start = (bf16[16,6,64,256]{3,2,1,0:T(8,128)(2,1)}, bf16[16,6,64,256]{3,2,1,0:T(8,128)(2,1)}, u32[]{:S(2)}, u32[]{:S(2)}) collective-permute-start(bf16[16,6,64,256]{3,2,1,0:T(8,128)(2,1)} %param.11), channel_id=1, source_target_pairs={{0,1},{1,2},{2,3},{3,0},{4,5},{5,6},{6,7},{7,4},{8,9},{9,10},{10,1... | collective-permute-start | bytes 9437192 | tf_op jit(solution)/shard_map/ppermute | solution.py:16
  13.7 367.8 %collective-permute-start.1 = (bf16[16,6,64,256]{3,2,1,0:T(8,128)(2,1)}, bf16[16,6,64,256]{3,2,1,0:T(8,128)(2,1)}, u32[]{:S(2)}, u32[]{:S(2)}) collective-permute-start(bf16[16,6,64,256]{3,2,1,0:T(8,128)(2,1)} %param.11), channel_id=1, source_target_pairs={{0,3},{1,0},{2,1},{3,2},{4,7},{5,4},{6,5},{7,6},{8,11},{9,8},{10,9... | collective-permute-start | bytes 9437192 | tf_op jit(solution)/shard_map/ppermute | solution.py:19
  108.8 276.7 %collective-permute-start.2 = (bf16[16,6,64,256]{3,2,1,0:T(8,128)(2,1)}, bf16[16,6,64,256]{3,2,1,0:T(8,128)(2,1)}, u32[]{:S(2)}, u32[]{:S(2)}) collective-permute-start(bf16[16,6,64,256]{3,2,1,0:T(8,128)(2,1)} %collective-permute-done), channel_id=1, source_target_pairs={{0,1},{1,2},{2,3},{3,0},{4,5},{5,6},{6,7},{7,4},{8,9},{9,10},{10,1... | collective-permute-start | bytes 9437192 | tf_op jit(solution)/shard_map/ppermute | solution.py:16
  310.6 0.8 copy-start.2
  338.8 0.8 copy-start.4
  369.5 6.2 copy-start.10
  427.0 4.1 copy-start
  516.1 2.0 copy-start.9
  516.2 2.7 copy-start.11
  518.9 2.9 copy-start.1
  553.8 176.0 %reduce-scatter.9.cloned.1.call-start = ((), (), s32[]{:S(2)}) async-start(), calls=%async_computation.11 | async-start | bytes 8257536 | tf_op jit(solution)/shard_map/reduce_scatter | solution.py:71
  608.4 135.1 %reduce-scatter.11.cloned.1.call-start = ((), (), s32[]{:S(2)}) async-start(), calls=%async_computation.14 | async-start | bytes 8257536 | tf_op jit(solution)/shard_map/reduce_scatter | solution.py:71
  663.3 294.4 %reduce-scatter.19.cloned.1.call-start = ((), (), s32[]{:S(2)}) async-start(), calls=%async_computation.18 | async-start | bytes 15728640 | tf_op jit(solution)/shard_map/reduce_scatter | solution.py:171
  692.2 480.6 %reduce-scatter.13.cloned.1.call-start = ((), (), s32[]{:S(2)}) async-start(), calls=%async_computation.15 | async-start | bytes 15728640 | tf_op jit(solution)/shard_map/reduce_scatter | solution.py:168
  720.9 3.8 copy-start.8
  720.9 499.8 %reduce-scatter.21.cloned.1.call-start = ((), (), s32[]{:S(2)}) async-start(), calls=%async_computation.19 | async-start | bytes 2621440 | tf_op jit(solution)/shard_map/reduce_scatter | solution.py:180
  724.6 519.8 %reduce-scatter.23.cloned.1.call-start = ((), (), s32[]{:S(2)}) async-start(), calls=%async_computation.20 | async-start | bytes 655360 | tf_op jit(solution)/shard_map/reduce_scatter | solution.py:183
  725.8 3.9 copy-start.5
  725.9 17.6 %copy-start.3 = (bf16[1024,256]{1,0:T(8,128)(2,1)S(1)}, bf16[1024,256]{1,0:T(8,128)(2,1)}, u32[]{:S(2)}) copy-start(bf16[1024,256]{1,0:T(8,128)(2,1)} %copy-done.2) | copy-start | bytes 1572868
  725.9 563.6 %reduce-scatter.17.cloned.1.call-start = ((), (), s32[]{:S(2)}) async-start(), calls=%async_computation.17 | async-start | bytes 2621440 | tf_op jit(solution)/shard_map/reduce_scatter | solution.py:177
Sparse Core Ops, SparseCore 0:
  9.9 37.2 all-gather.5
  48.8 86.3 all-gather.7
  136.8 74.0 all-gather.11
  212.6 58.6 all-gather.13
  272.7 233.3 all-gather.9
  553.9 19.0 reduce-scatter.14
  608.5 64.1 reduce-scatter.8
  676.5 66.9 reduce-scatter.10
  745.8 211.8 reduce-scatter.18
  959.9 212.8 reduce-scatter.12
  1175.7 44.9 reduce-scatter.20
  1223.5 20.9 reduce-scatter.22
  1247.4 42.0 reduce-scatter.16
